TPU v7x, 32 devices: a whole 2x2x4 slice. The times are simulated.
32 devices in a mesh: dp: 4 (over y, x), expert: 8 (over z, core).
Axes of the slice: x: 2, y: 2, z: 4, core: 2. Of those that a mesh axis runs over, the one named last changes fastest.
Arguments:
- tables: float32 [4, 8192, 256], P(None, ('dp', 'expert')), may hold values from -3 to 3
- accum: float32 [4, 8192], P(None, ('dp', 'expert')), may hold values from 0.01 to 1
- bag_owner: int32 [4096, 16], P(('dp', 'expert')), may hold values from 0 to 31, all different within a row; in each aligned block of 128 rows (0 to 127, 128 to 255, ...) at most 81 rows name the same one
- bag_row: int32 [4096, 16], P(('dp', 'expert')), may hold values from 0 to 255
- bag_len: int32 [4, 4096], P(None, ('dp', 'expert')), may hold values from 1 to 4, 10240 in all within a row
- route: int32 [4096, 2], P(('dp', 'expert')), may hold values from 0 to 7, all different within a row; in each aligned block of 128 rows (0 to 127, 128 to 255, ...) at most 33 rows name the same one
- labels: float32 [4096, 2], P(('dp', 'expert')), may hold values from 0 to 1
- w_in: bfloat16 [8, 1024, 2048], P('expert', None, 'dp'), may hold values from -0.1875 to 0.1875
- w_out: bfloat16 [8, 2048, 1024], P('expert', 'dp'), may hold values from -0.125 to 0.125
- gate_w: bfloat16 [2, 1024, 8], replicated, may hold values from -0.1875 to 0.1875
- head: float32 [2, 1024], replicated, may hold values from -0.375 to 0.375
Outputs:
- logits: float32 [4096, 2], P(('dp', 'expert'))
- new_tables: float32 [4, 8192, 256], P(None, ('dp', 'expert'))
- new_accum: float32 [4, 8192], P(None, ('dp', 'expert'))
Inputs may be any that keep to these rules, and one draw needn't show every extreme that they name: `bag_owner`: each sample names 16 different owners; the rows of one device name any one owner at most 81 times. `route`: each sample names two different experts; the rows of one device name any one expert at most 33 times.
All inputs are finite; a program needn't handle non-finite values. No bound on the sum of `bag_len` on one device may be relied on, other than what follows from the above.
Results may differ from a plain program's by a relative error of at most 0.0062.
Values may be sent and summed in bfloat16 or wider, within the bound.
No kernel may reach another device: no remote copies, remote signals or barrier semaphores. Data moves between devices by JAX's collectives and lax.ppermute only.
A program may use at most 128 MiB of HBM per device.

v0:
```python
import jax
import jax.numpy as jnp
from jax import lax
from jax.sharding import PartitionSpec as P

learn_rate = 0.3
norm_eps = 1e-05


def slot_rank(dest, buckets):
    count = dest.shape[0]
    order = jnp.argsort(dest, stable=True)
    ordered = dest[order]
    starts = jnp.searchsorted(ordered, jnp.arange(buckets, dtype=jnp.int32), side="left")
    within = jnp.arange(count, dtype=jnp.int32) - starts[ordered]
    return jnp.zeros((count,), jnp.int32).at[order].set(within)


def send_requests(requests):
    return lax.all_to_all(
        lax.all_to_all(requests, "expert", split_axis=2, concat_axis=2, tiled=True),
        "dp",
        split_axis=1,
        concat_axis=1,
        tiled=True,
    )


def send_rows(values):
    return lax.all_to_all(
        lax.all_to_all(values, "expert", split_axis=2, concat_axis=2, tiled=True),
        "dp",
        split_axis=1,
        concat_axis=1,
        tiled=True,
    )


def per_device(
    tables, accum, bag_owner, bag_row, bag_len, route, labels, w_in, w_out, gate_w, head
):
    dp_count = lax.axis_size("dp")
    expert_count = lax.axis_size("expert")
    device_count = dp_count * expert_count
    sample_count = route.shape[0]
    table_count = tables.shape[0]
    row_count = tables.shape[1]
    emb_width = tables.shape[2]
    bag_slots = bag_owner.shape[1] // table_count
    model_width = table_count * emb_width
    task_count = labels.shape[1]
    cap_rows = (5 * sample_count * table_count * bag_slots + 4 * device_count - 1) // (
        4 * device_count
    ) + 1
    cap_expert = (2 * sample_count + expert_count - 1) // expert_count + 1
    full_in, full_out = (
        lax.all_gather(w_in[0], "dp", axis=1, tiled=True),
        lax.all_gather(w_out[0], "dp", axis=0, tiled=True),
    )
    lookups = sample_count * table_count * bag_slots
    owners = bag_owner.reshape(-1)
    column = jnp.arange(lookups, dtype=jnp.int32) % (table_count * bag_slots)
    table_of = column // bag_slots
    owner_slot = slot_rank(owners, device_count)
    flat_row = table_of * row_count + bag_row.reshape(-1)
    requests = jnp.zeros((cap_rows, device_count), jnp.int32).at[owner_slot, owners].set(flat_row)
    wanted = send_requests(requests.reshape(cap_rows, dp_count, expert_count))
    flat_table = tables.reshape(table_count * row_count, emb_width)
    served = flat_table[wanted.reshape(-1)].reshape(cap_rows, dp_count, expert_count, emb_width)
    returned = send_rows(served).reshape(cap_rows * device_count, emb_width)
    fetched = returned[owner_slot * device_count + owners]
    live = (jnp.arange(bag_slots, dtype=jnp.int32)[None, None, :] < bag_len.T[:, :, None]).reshape(
        -1
    )
    masked = jnp.where(live[:, None], fetched, 0.0)
    pooled = jnp.sum(masked.reshape(sample_count, table_count, bag_slots, emb_width), axis=2)
    features = pooled.reshape(sample_count, model_width).astype(jnp.bfloat16)
    experts_flat = route.reshape(-1)
    expert_slot = slot_rank(experts_flat, expert_count)
    sample_of = jnp.arange(2 * sample_count, dtype=jnp.int32) // 2
    outgoing = (
        jnp.zeros((cap_expert, expert_count, model_width), jnp.bfloat16)
        .at[expert_slot, experts_flat]
        .set(features[sample_of])
    )
    arrived = lax.all_to_all(outgoing, "expert", split_axis=1, concat_axis=1, tiled=True)
    flat = arrived.reshape(-1, model_width)
    pre = jnp.dot(flat, full_in, preferred_element_type=jnp.float32)
    hidden = jnp.maximum(pre, 0.0).astype(jnp.bfloat16)
    result = jnp.dot(hidden, full_out, preferred_element_type=jnp.float32).astype(jnp.bfloat16)
    result = result.reshape(arrived.shape)
    saved_part = hidden.reshape(arrived.shape[0], arrived.shape[1], hidden.shape[1])
    back = lax.all_to_all(result, "expert", split_axis=1, concat_axis=1, tiled=True)
    picked = (
        back[expert_slot, experts_flat].reshape(sample_count, 2, model_width).astype(jnp.float32)
    )
    scores = jnp.einsum("sd,tde->ste", features, gate_w, preferred_element_type=jnp.float32)
    chosen = jnp.take_along_axis(
        scores, jnp.broadcast_to(route[:, None, :], (sample_count, task_count, 2)), axis=2
    )
    first = jax.nn.sigmoid(chosen[..., 0] - chosen[..., 1])
    gates = jnp.stack([first, 1.0 - first], axis=-1)
    combined = jnp.einsum("stk,skd->std", gates, picked, precision=lax.Precision.HIGHEST)
    scale = jnp.sqrt(jnp.mean(combined * combined, axis=-1, keepdims=True) + norm_eps)
    normed = combined / scale
    logits = jnp.sum(normed * head[None], axis=-1)
    dlogit = jax.nn.sigmoid(logits) - labels
    dnormed = dlogit[..., None] * head[None]
    dcomb = (dnormed - normed * jnp.mean(dnormed * normed, axis=-1, keepdims=True)) / scale
    dpicked = jnp.einsum("stk,std->skd", gates, dcomb, precision=lax.Precision.HIGHEST).astype(
        jnp.bfloat16
    )
    dgates = jnp.einsum("std,skd->stk", dcomb, picked, precision=lax.Precision.HIGHEST)
    ddelta = (dgates[..., 0] - dgates[..., 1]) * first * (1.0 - first)
    onehot = (route[:, :, None] == jnp.arange(expert_count, dtype=jnp.int32)[None, None, :]).astype(
        jnp.float32
    )
    dscores = ddelta[:, :, None] * (onehot[:, None, 0, :] - onehot[:, None, 1, :])
    dgate_in = jnp.einsum(
        "ste,tde->sd", dscores, gate_w.astype(jnp.float32), precision=lax.Precision.HIGHEST
    )
    grads_out = (
        jnp.zeros((cap_expert, expert_count, model_width), jnp.bfloat16)
        .at[expert_slot, experts_flat]
        .set(dpicked.reshape(-1, model_width))
    )
    arrived_grads = lax.all_to_all(grads_out, "expert", split_axis=1, concat_axis=1, tiled=True)
    flat_grads = arrived_grads.reshape(-1, model_width)
    dhidden = lax.dot_general(
        flat_grads, full_out, (((1,), (1,)), ((), ())), preferred_element_type=jnp.float32
    )
    active = saved_part.reshape(-1, full_in.shape[1]) > 0
    dpre = jnp.where(active, dhidden, 0.0).astype(jnp.bfloat16)
    dinput = lax.dot_general(
        dpre, full_in, (((1,), (1,)), ((), ())), preferred_element_type=jnp.float32
    )
    dinput = dinput.astype(jnp.bfloat16).reshape(arrived_grads.shape)
    back_grads = lax.all_to_all(dinput, "expert", split_axis=1, concat_axis=1, tiled=True)
    dexpert = (
        back_grads[expert_slot, experts_flat]
        .astype(jnp.float32)
        .reshape(sample_count, 2, model_width)
    )
    dfeatures = dgate_in + jnp.sum(dexpert, axis=1)
    dpooled = dfeatures.reshape(sample_count, table_count, emb_width)
    per_lookup = jnp.broadcast_to(
        dpooled[:, :, None, :], (sample_count, table_count, bag_slots, emb_width)
    ).reshape(lookups, emb_width)
    per_lookup = jnp.where(live[:, None], per_lookup, 0.0)
    grad_buffer = (
        jnp.zeros((cap_rows, device_count, emb_width), jnp.float32)
        .at[owner_slot, owners]
        .set(per_lookup)
    )
    arrived_rows = send_rows(grad_buffer.reshape(cap_rows, dp_count, expert_count, emb_width))
    row_grads = (
        jnp.zeros((table_count * row_count, emb_width), jnp.float32)
        .at[wanted.reshape(-1)]
        .add(arrived_rows.reshape(-1, emb_width))
    )
    row_grads = row_grads.reshape(table_count, row_count, emb_width)
    new_accum = accum + jnp.mean(row_grads * row_grads, axis=-1)
    new_tables = tables - learn_rate * row_grads / jnp.sqrt(new_accum)[..., None]
    return (logits, new_tables, new_accum)


def solution(mesh):
    in_specs = (
        P(None, ("dp", "expert"), None),
        P(None, ("dp", "expert")),
        P(("dp", "expert"), None),
        P(("dp", "expert"), None),
        P(None, ("dp", "expert")),
        P(("dp", "expert"), None),
        P(("dp", "expert"), None),
        P("expert", None, "dp"),
        P("expert", "dp", None),
        P(),
        P(),
    )
    out_specs = (
        P(("dp", "expert"), None),
        P(None, ("dp", "expert"), None),
        P(None, ("dp", "expert")),
    )
    return jax.shard_map(
        per_device, mesh=mesh, in_specs=in_specs, out_specs=out_specs, check_vma=False
    )
```

profile of v0, /device:TPU:0, one launch (start us, length us, event | category | flops | bytes accessed | tf_op | source)
XLA Modules:
  0.0 530.2 jit_solution(621122116833927265)
XLA Ops:
  7.9 0.8 copy.193
  8.8 5.0 sort.34
  13.9 11.8 %gather_fusion.2 = s32[2048]{0:T(1024)S(1)} fusion(s32[2048]{0:T(1024)S(1)} %reshape.277, s32[2048]{0:T(1024)S(1)} %get-tuple-element.251), kind=kCustom, calls=%fused_computation.2 | custom fusion | bytes 24576 | tf_op jit(solution)/shard_map/gather | solution.py:13
  25.7 9.0 %while.48 = (s32[]{:T(128)}, u32[32]{0:T(128)S(1)}, u32[32]{0:T(128)S(1)}, s32[2048]{0:T(1024)S(1)}, s32[]{:T(128)}, /*index=5*/s32[]{:T(128)}, s32[]{}) while((s32[]{:T(128)}, u32[32]{0:T(128)S(1)}, u32[32]{0:T(128)S(1)}, s32[2048]{0:T(1024)S(1)}, s32[]{:T(128)}, /*index=5*/s32[]{:T(128)}, s32[]{}) %tuple.144), condition=%wide.region_2.3_spmd.clone, body=%wide.region_1.2_spmd.clone.sunk | while | flops 1444 | bytes 5732 | solution.py:14
  34.8 0.7 fusion.94
  35.5 4.3 compare_select_fusion.3
  40.0 0.7 fusion.93
  41.4 15.6 %select_subtract_fusion = s32[2048]{0:T(1024)S(1)} fusion(pred[2048]{0:T(1024)(128)(4,1)S(1)} %get-tuple-element.214, pred[2048]{0:T(1024)(128)(4,1)S(1)} %get-tuple-element.213, pred[2048]{0:T(1024)(128)(4,1)S(1)} %get-tuple-element.212, pred[2048]{0:T(1024)(128)(4,1)S(1)} %get-tuple-element.211, pred[2048]{0:T(1024)(128)(4,1)S(1)} %get-tuple-element.210, ...), kind=kLoop, calls=%fused_computation.132 | loop fusion | flops 53248 | bytes 67684 | tf_op jit(solution)/shard_map/sub | solution.py:15
  57.0 8.0 %scatter_custom_fusion = s32[2048]{0:T(1024)S(1)} fusion(s32[2048]{0:T(1024)S(1)} %get-tuple-element.252, s32[2048]{0:T(1024)S(1)} %select_subtract_fusion, s32[]{:T(128)} %constant.134.clone.1), kind=kCustom, calls=%fused_computation.157 | custom fusion | bytes 8196 | tf_op jit(solution)/shard_map/scatter | solution.py:16
  65.9 8.1 %scatter_custom_fusion.5 = s32[2592]{0:T(1024)S(1)} fusion(s32[2048]{0:T(1024)S(1)} %get-tuple-element.254, s32[2048]{0:T(1024)S(1)} %get-tuple-element.297, s32[]{:T(128)} %constant.134.clone.1), kind=kCustom, calls=%fused_computation.143 | custom fusion | bytes 10372
  74.1 11.8 %all_to_all.50 = s32[81,4,8]{0,1,2:T(4,128)S(1)} all-to-all(s32[81,4,8]{0,1,2:T(4,128)S(1)} %copy.196), channel_id=1, replica_groups=mesh['dp'=4,'expert'=8] {'expert'}, dimensions={2} | all-to-all | bytes 20736 | tf_op jit(solution)/shard_map/all_to_all | solution.py:21
  85.9 8.2 %all_to_all.51 = s32[81,4,8]{0,2,1:T(8,128)S(1)} all-to-all(s32[81,4,8]{0,2,1:T(8,128)S(1)} %copy.197), channel_id=1, replica_groups=mesh['dp'=4,'expert'=8] {'dp'}, dimensions={1} | all-to-all | bytes 20736 | tf_op jit(solution)/shard_map/all_to_all | solution.py:20
  94.5 7.6 %gather_fusion.3 = f32[2592,256]{1,0:T(8,128)} fusion(f32[1024,256]{1,0:T(8,128)S(1)} %bitcast.129, s32[3072]{0:T(1024)S(1)} %pad_clamp_fusion.2), kind=kCustom, calls=%fused_computation.3 | custom fusion | bytes 5318784 | tf_op jit(solution)/shard_map/gather | solution.py:69
  102.1 4.4 copy.199
  106.5 4.6 all-to-all-start.2
  112.1 3.2 sort.35
  115.3 1.9 gather_fusion.5
  117.2 54.8 %all-to-all-done.2 = f32[81,4,8,256]{3,1,0,2:T(4,128)} async-done(((f32[81,4,8,256]{3,1,0,2:T(4,128)}), f32[81,4,8,256]{3,1,0,2:T(4,128)}, u32[]{:S(2)}, u32[]{:S(2)}) %all-to-all-start.2) | async-done | bytes 2654240 | tf_op jit(solution)/shard_map/all_to_all | solution.py:31
  172.0 3.9 copy.200
  175.9 4.6 all-to-all-start.3
  180.5 6.3 %while.49 = (s32[]{:T(128)}, u32[8]{0:T(128)S(1)}, u32[8]{0:T(128)S(1)}, s32[256]{0:T(256)S(1)}, s32[]{:T(128)}, /*index=5*/s32[]{:T(128)}, s32[]{}) while((s32[]{:T(128)}, u32[8]{0:T(128)S(1)}, u32[8]{0:T(128)S(1)}, s32[256]{0:T(256)S(1)}, s32[]{:T(128)}, /*index=5*/s32[]{:T(128)}, s32[]{}) %tuple.147), condition=%wide.region_8.9_spmd.clone, body=%wide.region_7.8_spmd.clone.sunk | while | flops 1132 | bytes 4580 | solution.py:14
  187.8 4.4 compare_select_fusion.15
  192.8 1.9 scatter_custom_fusion.1
  195.0 16.4 %all-to-all-done.3 = f32[81,4,8,256]{3,2,0,1:T(8,128)} async-done(((f32[81,4,8,256]{3,2,0,1:T(8,128)}), f32[81,4,8,256]{3,2,0,1:T(8,128)}, u32[]{:S(2)}, u32[]{:S(2)}) %all-to-all-start.3) | async-done | bytes 2654240 | tf_op jit(solution)/shard_map/all_to_all | solution.py:30
  211.4 3.7 copy.201
  215.1 8.4 %gather_fusion.4 = f32[2048,256]{1,0:T(8,128)S(1)} fusion(f32[2592,256]{1,0:T(8,128)} %bitcast.130, s32[2048]{0:T(1024)S(1)} %get-tuple-element.249), kind=kCustom, calls=%fused_computation.4 | custom fusion | bytes 4202496 | tf_op jit(solution)/shard_map/gather | solution.py:71
  223.5 1.7 gather.54
  225.2 3.0 select_reduce_fusion
  228.3 1.2 gather_fusion.6
  229.5 16.0 %scatter_fusion = bf16[33,8,1024]{2,1,0:T(8,128)(2,1)S(1)} fusion(bf16[33,8,1024]{2,1,0:T(8,128)(2,1)S(1)} %broadcast.283.clone, s32[256]{0:T(256)S(1)} %bitcast.133, bf16[256,1024]{1,0:T(8,128)(2,1)S(1)} %gather_fusion.6), kind=kCustom, calls=%fused_computation.12 | custom fusion | bytes 1574912 | tf_op jit(solution)/shard_map/scatter | solution.py:84
  245.5 1.1 copy.206
  246.6 3.5 all-to-all-start.4
  250.2 18.0 %all-to-all-done.4 = bf16[33,8,1024]{2,0,1:T(8,128)(2,1)S(1)} async-done(((bf16[33,8,1024]{2,0,1:T(8,128)(2,1)}), bf16[33,8,1024]{2,0,1:T(8,128)(2,1)S(1)}, u32[]{:S(2)}, u32[]{:S(2)}) %all-to-all-start.4) | async-done | bytes 540704 | tf_op jit(solution)/shard_map/all_to_all | solution.py:86
  268.3 3.6 fusion.25
  271.9 3.9 fusion.37
  275.8 1.1 copy.208
  277.0 3.7 all-to-all-start.5
  281.2 3.4 gather_fusion.9
  285.1 13.6 %all-to-all-done.5 = bf16[33,8,1024]{2,0,1:T(8,128)(2,1)S(1)} async-done(((bf16[33,8,1024]{2,0,1:T(8,128)(2,1)}), bf16[33,8,1024]{2,0,1:T(8,128)(2,1)S(1)}, u32[]{:S(2)}, u32[]{:S(2)}) %all-to-all-start.5) | async-done | bytes 540704 | tf_op jit(solution)/shard_map/all_to_all | solution.py:93
  299.0 2.7 gather_fusion.7
  302.0 2.7 multiply_reduce_fusion.2
  304.8 0.7 multiply_reduce_fusion.1
  306.9 0.9 fusion.45
  307.7 3.8 convolution_convert_fusion
  311.8 16.0 %scatter_fusion.1 = bf16[33,8,1024]{2,1,0:T(8,128)(2,1)S(1)} fusion(bf16[33,8,1024]{2,1,0:T(8,128)(2,1)S(1)} %broadcast.283, s32[256]{0:T(256)S(1)} %bitcast.134, bf16[256,1024]{1,0:T(8,128)(2,1)S(1)} %reshape.457), kind=kCustom, calls=%fused_computation.13 | custom fusion | bytes 1574912 | tf_op jit(solution)/shard_map/scatter | solution.py:125
  327.8 1.1 copy.216
  328.9 3.5 all-to-all-start.6
  332.7 17.8 %all-to-all-done.6 = bf16[33,8,1024]{2,0,1:T(8,128)(2,1)S(1)} async-done(((bf16[33,8,1024]{2,0,1:T(8,128)(2,1)}), bf16[33,8,1024]{2,0,1:T(8,128)(2,1)S(1)}, u32[]{:S(2)}, u32[]{:S(2)}) %all-to-all-start.6) | async-done | bytes 540704 | tf_op jit(solution)/shard_map/all_to_all | solution.py:127
  350.5 6.4 %fusion.40 = bf16[33,8,1024]{2,1,0:T(8,128)(2,1)S(1)} fusion(bf16[1,1024,2048]{2,1,0:T(8,128)(2,1)} %all-gather.5.cloned.1.call-done, bf16[1,2048,1024]{2,1,0:T(8,128)(2,1)} %all-gather.7.cloned.1.call-done, bf16[264,2048]{1,0:T(8,128)(2,1)} %copy-done.13, bf16[33,8,1024]{2,0,1:T(8,128)(2,1)S(1)} %all-to-all-done.6), kind=kOutput, calls=%fused_computation.55 | convolution fusion | flops 2216484864 | bytes 10551296 | tf_op jit(solution)/shard_map/dot_general | solution.py:134
  356.9 1.1 copy.218
  358.1 3.8 all-to-all-start.7
  361.9 5.0 fusion.95
  367.2 12.7 %all-to-all-done.7 = bf16[33,8,1024]{2,0,1:T(8,128)(2,1)S(1)} async-done(((bf16[33,8,1024]{2,0,1:T(8,128)(2,1)}), bf16[33,8,1024]{2,0,1:T(8,128)(2,1)S(1)}, u32[]{:S(2)}, u32[]{:S(2)}) %all-to-all-start.7) | async-done | bytes 540704 | tf_op jit(solution)/shard_map/all_to_all | solution.py:138
  380.2 2.7 gather_fusion.8
  383.5 1.2 reduce_sum.58
  385.5 2.0 broadcast_in_dim.146
  387.5 2.0 reshape.292
  389.5 12.2 %scatter_custom_fusion.6 = f32[2592,256]{1,0:T(8,128)} fusion(s32[2048]{0:T(1024)} %get-tuple-element.253, f32[2048,256]{1,0:T(8,128)S(1)} %reshape.292, f32[]{:T(128)} %constant.151.clone.1, pred[2048]{0:T(1024)(128)(4,1)S(1)} %lt.149), kind=kCustom, calls=%fused_computation.45 | custom fusion | flops 524288 | bytes 4754432
  401.7 2.8 copy.220
  404.4 63.4 %all_to_all.52 = f32[81,4,8,256]{3,1,0,2:T(4,128)S(1)} all-to-all(f32[81,4,8,256]{3,1,0,2:T(4,128)S(1)} %copy.220), channel_id=1, replica_groups=mesh['dp'=4,'expert'=8] {'expert'}, dimensions={2} | all-to-all | bytes 5308416 | tf_op jit(solution)/shard_map/all_to_all | solution.py:31
  468.3 34.5 %all_to_all.53 = f32[81,4,8,256]{3,2,0,1:T(8,128)S(1)} all-to-all(f32[81,4,8,256]{3,2,0,1:T(8,128)S(1)} %copy.221), channel_id=1, replica_groups=mesh['dp'=4,'expert'=8] {'dp'}, dimensions={1} | all-to-all | bytes 5308416 | tf_op jit(solution)/shard_map/all_to_all | solution.py:30
  502.8 1.9 copy.222
  504.7 16.1 %scatter_custom_fusion.4 = f32[1024,256]{1,0:T(8,128)S(1)} fusion(s32[2592]{0:T(1024)S(1)} %fusion.60, f32[2592,256]{1,0:T(8,128)} %bitcast.140, f32[]{:T(128)} %constant.151.clone.1), kind=kCustom, calls=%fused_computation.73 | custom fusion | flops 663552 | bytes 1049088 | tf_op jit(solution)/shard_map/scatter-add | solution.py:159
  521.7 1.2 divide_subtract_fusion
  (198 shorter events, 27.5 us)
Async XLA Ops:
  7.2 273.9 %copy-start = (bf16[2,1024,8]{1,2,0:T(8,128)(2,1)S(1)}, bf16[2,1024,8]{1,2,0:T(8,128)(2,1)}, u32[]{:S(2)}) copy-start(bf16[2,1024,8]{1,2,0:T(8,128)(2,1)} %param.24) | copy-start | bytes 98308
  7.2 243.0 %all-gather.5.cloned.1.call-start = ((), (), s32[]{:S(2)}) async-start(), calls=%async_computation.10 | async-start | bytes 5242880 | tf_op jit(solution)/shard_map/all_gather | solution.py:57
  13.9 26.0 %copy-start.5 = (s32[128,16]{0,1:T(8,128)S(1)}, s32[128,16]{0,1:T(8,128)}, u32[]{:S(2)}) copy-start(s32[128,16]{0,1:T(8,128)} %param.18) | copy-start | bytes 24580
  25.7 39.4 %copy-start.12 = (s32[2]{0:T(128)S(1)}, s32[2]{0:T(128)}, u32[]{:S(2)}) copy-start(s32[2]{0:T(128)} %constant.166) | copy-start | bytes 28
  25.7 39.5 %copy-start.10 = (s32[2]{0:T(128)S(1)}, s32[2]{0:T(128)}, u32[]{:S(2)}) copy-start(s32[2]{0:T(128)} %constant.163) | copy-start | bytes 28
  25.7 39.5 %copy-start.11 = (s32[2]{0:T(128)S(1)}, s32[2]{0:T(128)}, u32[]{:S(2)}) copy-start(s32[2]{0:T(128)} %constant.169) | copy-start | bytes 28
  25.7 68.8 %copy-start.1 = (f32[4,256,256]{2,1,0:T(8,128)S(1)}, f32[4,256,256]{2,1,0:T(8,128)}, u32[]{:S(2)}) copy-start(f32[4,256,256]{2,1,0:T(8,128)} %param.15) | copy-start | bytes 3145732
  106.5 5.3 %copy-start.4 = (s32[128,2]{0,1:T(2,128)S(1)}, s32[128,2]{0,1:T(2,128)}, u32[]{:S(2)}) copy-start(s32[128,2]{0,1:T(2,128)} %param.20) | copy-start | bytes 3076
  106.5 65.5 %all-to-all-start.2 = ((f32[81,4,8,256]{3,1,0,2:T(4,128)}), f32[81,4,8,256]{3,1,0,2:T(4,128)}, u32[]{:S(2)}, u32[]{:S(2)}) async-start(f32[81,4,8,256]{3,1,0,2:T(4,128)} %copy.199), calls=%async_computation.2 | async-start | bytes 5308416 | tf_op jit(solution)/shard_map/all_to_all | solution.py:31
  111.1 160.9 %all-gather.7.cloned.1.call-start = ((), (), s32[]{:S(2)}) async-start(), calls=%async_computation.11 | async-start | bytes 5242880 | tf_op jit(solution)/shard_map/all_gather | solution.py:58
  175.9 35.5 %all-to-all-start.3 = ((f32[81,4,8,256]{3,2,0,1:T(8,128)}), f32[81,4,8,256]{3,2,0,1:T(8,128)}, u32[]{:S(2)}, u32[]{:S(2)}) async-start(f32[81,4,8,256]{3,2,0,1:T(8,128)} %copy.200), calls=%async_computation.3 | async-start | bytes 5308416 | tf_op jit(solution)/shard_map/all_to_all | solution.py:30
  180.5 6.5 %copy-start.8 = (s32[4,128]{1,0:T(4,128)S(1)}, s32[4,128]{1,0:T(4,128)}, u32[]{:S(2)}) copy-start(s32[4,128]{1,0:T(4,128)} %param.19) | copy-start | bytes 6148
  246.6 21.6 %all-to-all-start.4 = ((bf16[33,8,1024]{2,0,1:T(8,128)(2,1)}), bf16[33,8,1024]{2,0,1:T(8,128)(2,1)S(1)}, u32[]{:S(2)}, u32[]{:S(2)}) async-start(bf16[33,8,1024]{2,0,1:T(8,128)(2,1)} %copy.206), calls=%async_computation.4 | async-start | bytes 1310720 | tf_op jit(solution)/shard_map/all_to_all | solution.py:86
  271.9 3.9 copy-start.13
  277.0 21.8 %all-to-all-start.5 = ((bf16[33,8,1024]{2,0,1:T(8,128)(2,1)}), bf16[33,8,1024]{2,0,1:T(8,128)(2,1)S(1)}, u32[]{:S(2)}, u32[]{:S(2)}) async-start(bf16[33,8,1024]{2,0,1:T(8,128)(2,1)} %copy.208), calls=%async_computation.5 | async-start | bytes 1310720 | tf_op jit(solution)/shard_map/all_to_all | solution.py:93
  301.7 3.0 copy-start.3
  301.9 2.8 copy-start.2
  302.0 3.6 copy-start.9
  305.6 0.6 copy-start.6
  328.9 21.6 %all-to-all-start.6 = ((bf16[33,8,1024]{2,0,1:T(8,128)(2,1)}), bf16[33,8,1024]{2,0,1:T(8,128)(2,1)S(1)}, u32[]{:S(2)}, u32[]{:S(2)}) async-start(bf16[33,8,1024]{2,0,1:T(8,128)(2,1)} %copy.216), calls=%async_computation.6 | async-start | bytes 1310720 | tf_op jit(solution)/shard_map/all_to_all | solution.py:127
  358.1 21.8 %all-to-all-start.7 = ((bf16[33,8,1024]{2,0,1:T(8,128)(2,1)}), bf16[33,8,1024]{2,0,1:T(8,128)(2,1)S(1)}, u32[]{:S(2)}, u32[]{:S(2)}) async-start(bf16[33,8,1024]{2,0,1:T(8,128)(2,1)} %copy.218), calls=%async_computation.7 | async-start | bytes 1310720 | tf_op jit(solution)/shard_map/all_to_all | solution.py:138
  504.7 16.4 %copy-start.7 = (f32[4,256]{1,0:T(4,128)S(1)}, f32[4,256]{1,0:T(4,128)}, u32[]{:S(2)}) copy-start(f32[4,256]{1,0:T(4,128)} %param.16) | copy-start | bytes 12292
Sparse Core Ops, SparseCore 0:
  9.8 55.1 all-gather.4
  113.7 52.0 all-gather.6
where the time goes:
time: 539 us; the launch traced here: 530 us
  local copies, waits for them, and re-layouts  140 us (26%)
  waiting for transfers between devices  135 us (25%)
  blocking collectives  118 us (22%)
  other arithmetic  72.4 us (13%)
  matrix products  26 us (5%)
  starting transfers between devices  23.8 us (4%)
  between operations  15.3 us (3%)
    all_to_all x1, blocking collectives, send_rows(): lax.all_to_all(values, 'expert', split_axis=2, concat_axis=2, tiled=True)  63.4 us
    all_to_all x1, waiting for transfers between devices, send_rows(): lax.all_to_all(values, 'expert', split_axis=2, concat_axis=2, tiled=True)  54.8 us
    all_to_all x1, blocking collectives, send_rows(): lax.all_to_all(lax.all_to_all(values, 'expert', split_axis=2, concat_axis...  34.5 us
    all_to_all x1, waiting for transfers between devices, per_device(): lax.all_to_all(outgoing, 'expert', split_axis=1, concat_axis=1, tiled=True)  18 us
    all_to_all x1, waiting for transfers between devices, per_device(): lax.all_to_all(grads_out, 'expert', split_axis=1, concat_axis=1, tiled=True)  17.8 us
    scatter x2, local copies, waits for them, and re-layouts, per_device(): grads_out = jnp.zeros((cap_expert, expert_count, model_width), jnp.bfloat...  17.1 us
    scatter x2, local copies, waits for them, and re-layouts, per_device(): outgoing = jnp.zeros((cap_expert, expert_count, model_width), jnp.bfloat1...  17.1 us
    all_to_all x1, waiting for transfers between devices, send_rows(): lax.all_to_all(lax.all_to_all(values, 'expert', split_axis=2, concat_axis...  16.4 us
  transfers between devices with their start and end apart: 8, of which 6 were waited for; matrix products, arithmetic and copies ran while one was open for 28% of the time, Pallas kernels for 0%

commit v1 on v0

--- a/solution.py
+++ b/solution.py
@@ -28,7 +28,12 @@
 
 def send_rows(values):
     return lax.all_to_all(
-        lax.all_to_all(values, "expert", split_axis=2, concat_axis=2, tiled=True),
+        jnp.concatenate(
+            lax.all_to_all(
+                jnp.stack(jnp.split(values, lax.axis_size("expert"), axis=2)), "expert", 0, 0
+            ),
+            axis=2,
+        ),
         "dp",
         split_axis=1,
         concat_axis=1,

time: 539 us -> 563 us (1.045)
  local copies, waits for them, and re-layouts: 140 us -> 175 us
  waiting for transfers between devices: 135 us -> 126 us
  blocking collectives: 118 us -> 110 us
    unnamed x37 -> x57, local copies, waits for them, and re-layouts: 9.93 us -> 25.7 us
    scatter x2, local copies, waits for them, and re-layouts: 9.97 us -> 23.3 us  [slot_rank(): return jnp.zeros((count,), jnp.int32).at[order].set(within)]
    split x0 -> x1, local copies, waits for them, and re-layouts: none -> 10.7 us  [send_rows(): jnp.split(values, lax.axis_size('expert'), axis=2)]
    all_to_all x3 -> x2, blocking collectives: 106 us -> 97.9 us  [the longest x1 63.4 us: send_rows(): lax.all_to_all(jnp.stack(jnp.split(values, lax.axis_size('expert'), axis=...]
    all_to_all x2 -> x3, waiting for transfers between devices: 71.2 us -> 63.5 us  [the longest x1 54.8 us: send_rows(): lax.all_to_all(jnp.stack(jnp.split(values, lax.axis_size('expert'), axis=...]
    all_to_all x2 -> x3, starting transfers between devices: 9.17 us -> 12.9 us  [the longest x1 4.61 us: send_rows(): lax.all_to_all(jnp.concatenate(lax.all_to_all(jnp.stack(jnp.split(values,...]
  transfers between devices with their start and end apart: 8 -> 9, of which waited for: 6 -> 7; matrix products, arithmetic and copies ran while one was open for 28% -> 20% of each run, Pallas kernels for 0% -> 0%
where the time goes in v1:
time: 563 us; the launch traced here: 553 us
  local copies, waits for them, and re-layouts  175 us (31%)
  waiting for transfers between devices  126 us (22%)
  blocking collectives  110 us (20%)
  other arithmetic  72.6 us (13%)
  starting transfers between devices  28.5 us (5%)
  matrix products  25.9 us (5%)
  between operations  15.2 us (3%)
    all_to_all x1, blocking collectives, send_rows(): lax.all_to_all(jnp.stack(jnp.split(values, lax.axis_size('expert'), axis=...  63.4 us
    all_to_all x1, waiting for transfers between devices, send_rows(): lax.all_to_all(jnp.stack(jnp.split(values, lax.axis_size('expert'), axis=...  54.8 us
    all_to_all x1, blocking collectives, send_rows(): lax.all_to_all(jnp.concatenate(lax.all_to_all(jnp.stack(jnp.split(values,...  34.5 us
    unnamed x57, local copies, waits for them, and re-layouts  25.7 us
    scatter x2, local copies, waits for them, and re-layouts, slot_rank(): return jnp.zeros((count,), jnp.int32).at[order].set(within)  23.3 us
    all_to_all x1, waiting for transfers between devices, per_device(): lax.all_to_all(outgoing, 'expert', split_axis=1, concat_axis=1, tiled=True)  18.1 us
    all_to_all x1, waiting for transfers between devices, per_device(): lax.all_to_all(grads_out, 'expert', split_axis=1, concat_axis=1, tiled=True)  17.8 us
    scatter x2, local copies, waits for them, and re-layouts, per_device(): outgoing = jnp.zeros((cap_expert, expert_count, model_width), jnp.bfloat1...  17.1 us
  transfers between devices with their start and end apart: 9, of which 7 were waited for; matrix products, arithmetic and copies ran while one was open for 20% of the time, Pallas kernels for 0%

profile of v1, /device:TPU:0, one launch (start us, length us, event | category | flops | bytes accessed | tf_op | source)
XLA Modules:
  0.0 553.4 jit_solution(3175806261251121657)
XLA Ops:
  8.1 5.0 sort.34
  13.1 11.8 %gather_fusion.2 = s32[2048]{0:T(1024)S(1)} fusion(s32[2048]{0:T(1024)S(1)} %reshape.289, s32[2048]{0:T(1024)S(1)} %get-tuple-element.259), kind=kCustom, calls=%fused_computation.2 | custom fusion | bytes 24576 | tf_op jit(solution)/shard_map/gather | solution.py:13
  25.0 9.0 %while.48 = (s32[]{:T(128)}, u32[32]{0:T(128)S(1)}, u32[32]{0:T(128)S(1)}, s32[2048]{0:T(1024)S(1)}, s32[]{:T(128)}, /*index=5*/s32[]{:T(128)}, s32[]{}) while((s32[]{:T(128)}, u32[32]{0:T(128)S(1)}, u32[32]{0:T(128)S(1)}, s32[2048]{0:T(1024)S(1)}, s32[]{:T(128)}, /*index=5*/s32[]{:T(128)}, s32[]{}) %tuple.152), condition=%wide.region_2.3_spmd.clone, body=%wide.region_1.2_spmd.clone.sunk | while | flops 1444 | bytes 5732 | solution.py:14
  35.6 4.3 compare_select_fusion.3
  40.5 15.8 %select_subtract_fusion = s32[2048]{0:T(1024)S(1)} fusion(pred[2048]{0:T(1024)(128)(4,1)S(1)} %get-tuple-element.214, pred[2048]{0:T(1024)(128)(4,1)S(1)} %get-tuple-element.213, pred[2048]{0:T(1024)(128)(4,1)S(1)} %get-tuple-element.212, pred[2048]{0:T(1024)(128)(4,1)S(1)} %get-tuple-element.211, pred[2048]{0:T(1024)(128)(4,1)S(1)} %get-tuple-element.210, ...), kind=kLoop, calls=%fused_computation.164 | loop fusion | flops 53248 | bytes 67684 | tf_op jit(solution)/shard_map/sub | solution.py:15
  56.2 8.0 %scatter_custom_fusion = s32[2048]{0:T(1024)S(1)} fusion(s32[2048]{0:T(1024)S(1)} %get-tuple-element.260, s32[2048]{0:T(1024)S(1)} %select_subtract_fusion, s32[]{:T(128)} %constant.134.clone.1), kind=kCustom, calls=%fused_computation.189 | custom fusion | bytes 8196 | tf_op jit(solution)/shard_map/scatter | solution.py:16
  65.4 8.1 %scatter_custom_fusion.5 = s32[2592]{0:T(1024)S(1)} fusion(s32[2048]{0:T(1024)S(1)} %get-tuple-element.262, s32[2048]{0:T(1024)S(1)} %get-tuple-element.307, s32[]{:T(128)} %constant.134.clone.1), kind=kCustom, calls=%fused_computation.175 | custom fusion | bytes 10372
  73.6 11.8 %all_to_all.50 = s32[81,4,8]{0,1,2:T(4,128)S(1)} all-to-all(s32[81,4,8]{0,1,2:T(4,128)S(1)} %copy.246), channel_id=1, replica_groups=mesh['dp'=4,'expert'=8] {'expert'}, dimensions={2} | all-to-all | bytes 20736 | tf_op jit(solution)/shard_map/all_to_all | solution.py:21
  86.0 3.7 all-to-all-start.1
  90.4 4.0 all-to-all-done.1
  94.8 7.6 %gather_fusion.3 = f32[2592,256]{1,0:T(8,128)} fusion(f32[1024,256]{1,0:T(8,128)S(1)} %bitcast.199, s32[3072]{0:T(1024)S(1)} %pad_clamp_fusion.2), kind=kCustom, calls=%fused_computation.3 | custom fusion | bytes 5318784 | tf_op jit(solution)/shard_map/gather | solution.py:74
  102.4 10.7 %fusion.107 = (f32[81,4,1,256]{3,2,1,0:T(1,128)S(1)}, f32[81,4,1,256]{3,2,1,0:T(1,128)S(1)}, f32[81,4,1,256]{3,2,1,0:T(1,128)S(1)}, f32[81,4,1,256]{3,2,1,0:T(1,...) fusion(f32[81,4,8,256]{3,2,1,0:T(8,128)} %bitcast.215), kind=kLoop, calls=%fused_computation.228 | loop fusion | bytes 5308416 | tf_op jit(solution)/shard_map/split | solution.py:33
  119.6 4.6 all-to-all-start.2
  125.3 3.2 sort.35
  128.5 1.9 gather_fusion.5
  130.4 54.8 %all-to-all-done.2 = f32[8,81,4,1,256]{4,2,3,1,0:T(4,128)} async-done(((f32[8,81,4,1,256]{4,2,3,1,0:T(4,128)}), f32[8,81,4,1,256]{4,2,3,1,0:T(4,128)}, u32[]{:S(2)}, u32[]{:S(2)}) %all-to-all-start.2) | async-done | bytes 2654240 | tf_op jit(solution)/shard_map/all_to_all | solution.py:32
  185.2 3.9 copy.257
  189.0 4.6 all-to-all-start.3
  193.7 6.3 %while.49 = (s32[]{:T(128)}, u32[8]{0:T(128)S(1)}, u32[8]{0:T(128)S(1)}, s32[256]{0:T(256)S(1)}, s32[]{:T(128)}, /*index=5*/s32[]{:T(128)}, s32[]{}) while((s32[]{:T(128)}, u32[8]{0:T(128)S(1)}, u32[8]{0:T(128)S(1)}, s32[256]{0:T(256)S(1)}, s32[]{:T(128)}, /*index=5*/s32[]{:T(128)}, s32[]{}) %tuple.155), condition=%wide.region_8.9_spmd.clone, body=%wide.region_7.8_spmd.clone.sunk | while | flops 1132 | bytes 4580 | solution.py:14
  201.0 4.4 compare_select_fusion.15
  206.0 15.3 %scatter_custom_fusion.1 = s32[256]{0:T(256)S(1)} fusion(s32[256]{0:T(256)S(1)} %compare_select_fusion.22, s32[256]{0:T(256)S(1)} %select_subtract_fusion.1, s32[]{:T(128)} %constant.134.clone.1), kind=kCustom, calls=%fused_computation.220 | custom fusion | bytes 1028 | tf_op jit(solution)/shard_map/scatter | solution.py:16
  221.5 4.7 all-to-all-done.3
  226.2 3.7 copy.258
  230.0 8.4 %gather_fusion.4 = f32[2048,256]{1,0:T(8,128)S(1)} fusion(f32[2592,256]{1,0:T(8,128)} %bitcast.200, s32[2048]{0:T(1024)S(1)} %get-tuple-element.257), kind=kCustom, calls=%fused_computation.4 | custom fusion | bytes 4202496 | tf_op jit(solution)/shard_map/gather | solution.py:76
  238.3 1.7 gather.54
  240.1 3.0 select_reduce_fusion
  243.1 1.2 gather_fusion.6
  244.3 16.0 %scatter_fusion = bf16[33,8,1024]{2,1,0:T(8,128)(2,1)S(1)} fusion(bf16[33,8,1024]{2,1,0:T(8,128)(2,1)S(1)} %broadcast.283.clone, s32[256]{0:T(256)S(1)} %bitcast.203, bf16[256,1024]{1,0:T(8,128)(2,1)S(1)} %gather_fusion.6), kind=kCustom, calls=%fused_computation.12 | custom fusion | bytes 1574912 | tf_op jit(solution)/shard_map/scatter | solution.py:89
  260.3 1.1 copy.263
  261.5 4.6 all-to-all-start.4
  266.1 18.1 %all-to-all-done.4 = bf16[33,8,1024]{2,0,1:T(8,128)(2,1)S(1)} async-done(((bf16[33,8,1024]{2,0,1:T(8,128)(2,1)}), bf16[33,8,1024]{2,0,1:T(8,128)(2,1)S(1)}, u32[]{:S(2)}, u32[]{:S(2)}) %all-to-all-start.4) | async-done | bytes 540704 | tf_op jit(solution)/shard_map/all_to_all | solution.py:91
  284.2 3.6 fusion.25
  287.9 3.9 fusion.37
  291.8 1.1 copy.265
  292.9 3.5 all-to-all-start.5
  297.0 3.4 gather_fusion.9
  301.5 13.0 %all-to-all-done.5 = bf16[33,8,1024]{2,0,1:T(8,128)(2,1)S(1)} async-done(((bf16[33,8,1024]{2,0,1:T(8,128)(2,1)}), bf16[33,8,1024]{2,0,1:T(8,128)(2,1)S(1)}, u32[]{:S(2)}, u32[]{:S(2)}) %all-to-all-start.5) | async-done | bytes 540704 | tf_op jit(solution)/shard_map/all_to_all | solution.py:98
  314.9 2.7 gather_fusion.7
  317.8 2.7 multiply_reduce_fusion.2
  322.7 0.8 fusion.45
  323.5 3.8 convolution_convert_fusion
  327.6 16.0 %scatter_fusion.1 = bf16[33,8,1024]{2,1,0:T(8,128)(2,1)S(1)} fusion(bf16[33,8,1024]{2,1,0:T(8,128)(2,1)S(1)} %broadcast.283, s32[256]{0:T(256)S(1)} %bitcast.204, bf16[256,1024]{1,0:T(8,128)(2,1)S(1)} %reshape.473), kind=kCustom, calls=%fused_computation.13 | custom fusion | bytes 1574912 | tf_op jit(solution)/shard_map/scatter | solution.py:130
  343.6 1.1 copy.273
  344.7 3.5 all-to-all-start.6
  348.5 17.8 %all-to-all-done.6 = bf16[33,8,1024]{2,0,1:T(8,128)(2,1)S(1)} async-done(((bf16[33,8,1024]{2,0,1:T(8,128)(2,1)}), bf16[33,8,1024]{2,0,1:T(8,128)(2,1)S(1)}, u32[]{:S(2)}, u32[]{:S(2)}) %all-to-all-start.6) | async-done | bytes 540704 | tf_op jit(solution)/shard_map/all_to_all | solution.py:132
  366.4 6.4 %fusion.40 = bf16[33,8,1024]{2,1,0:T(8,128)(2,1)S(1)} fusion(bf16[1,1024,2048]{2,1,0:T(8,128)(2,1)} %all-gather.5.cloned.1.call-done, bf16[1,2048,1024]{2,1,0:T(8,128)(2,1)} %all-gather.7.cloned.1.call-done, bf16[264,2048]{1,0:T(8,128)(2,1)} %copy-done.16, bf16[33,8,1024]{2,0,1:T(8,128)(2,1)S(1)} %all-to-all-done.6), kind=kOutput, calls=%fused_computation.55 | convolution fusion | flops 2216484864 | bytes 10551296 | tf_op jit(solution)/shard_map/dot_general | solution.py:139
  372.7 1.1 copy.275
  373.9 3.8 all-to-all-start.7
  377.8 5.0 fusion.112
  383.1 12.4 %all-to-all-done.7 = bf16[33,8,1024]{2,0,1:T(8,128)(2,1)S(1)} async-done(((bf16[33,8,1024]{2,0,1:T(8,128)(2,1)}), bf16[33,8,1024]{2,0,1:T(8,128)(2,1)S(1)}, u32[]{:S(2)}, u32[]{:S(2)}) %all-to-all-start.7) | async-done | bytes 540704 | tf_op jit(solution)/shard_map/all_to_all | solution.py:143
  395.8 2.7 gather_fusion.8
  399.2 1.3 reduce_sum.58
  401.1 2.0 broadcast_in_dim.146
  403.1 2.0 reshape.306
  405.1 12.1 %scatter_custom_fusion.6 = f32[2592,256]{1,0:T(8,128)} fusion(s32[2048]{0:T(1024)} %get-tuple-element.261, f32[2048,256]{1,0:T(8,128)S(1)} %reshape.306, f32[]{:T(128)} %constant.151.clone.1, pred[2048]{0:T(1024)(128)(4,1)S(1)} %lt.149), kind=kCustom, calls=%fused_computation.45 | custom fusion | flops 524288 | bytes 4754432
  417.3 2.1 fusion.66
  419.4 2.1 fusion.65
  421.5 2.1 fusion.64
  423.6 2.1 fusion.63
  427.9 63.4 %all_to_all.51 = f32[8,81,4,1,256]{4,2,1,3,0:T(4,128)S(1)} all-to-all(f32[8,81,4,1,256]{4,2,1,3,0:T(4,128)S(1)} %copy.277), channel_id=1, replica_groups=mesh['dp'=4,'expert'=8] {'expert'}, dimensions={0} | all-to-all | bytes 5308416 | tf_op jit(solution)/shard_map/all_to_all | solution.py:32
  491.8 34.5 %all_to_all.52 = f32[81,4,8,256]{3,2,0,1:T(8,128)S(1)} all-to-all(f32[81,4,8,256]{3,2,0,1:T(8,128)S(1)} %copy.278), channel_id=1, replica_groups=mesh['dp'=4,'expert'=8] {'dp'}, dimensions={1} | all-to-all | bytes 5308416 | tf_op jit(solution)/shard_map/all_to_all | solution.py:30
  526.2 1.9 copy.279
  528.2 16.1 %scatter_custom_fusion.4 = f32[1024,256]{1,0:T(8,128)S(1)} fusion(s32[2592]{0:T(1024)S(1)} %fusion.76, f32[2592,256]{1,0:T(8,128)} %bitcast.218, f32[]{:T(128)} %constant.151.clone.1), kind=kCustom, calls=%fused_computation.73 | custom fusion | flops 663552 | bytes 1049088 | tf_op jit(solution)/shard_map/scatter-add | solution.py:164
  545.2 1.2 divide_subtract_fusion
  (220 shorter events, 40.4 us)
Async XLA Ops:
  7.2 289.7 %copy-start = (bf16[2,1024,8]{1,2,0:T(8,128)(2,1)S(1)}, bf16[2,1024,8]{1,2,0:T(8,128)(2,1)}, u32[]{:S(2)}) copy-start(bf16[2,1024,8]{1,2,0:T(8,128)(2,1)} %param.24) | copy-start | bytes 98308
  24.9 39.4 %copy-start.8 = (s32[128,16]{0,1:T(8,128)S(1)}, s32[128,16]{0,1:T(8,128)}, u32[]{:S(2)}) copy-start(s32[128,16]{0,1:T(8,128)} %param.18) | copy-start | bytes 24580
  24.9 39.6 %copy-start.15 = (s32[2]{0:T(128)S(1)}, s32[2]{0:T(128)}, u32[]{:S(2)}) copy-start(s32[2]{0:T(128)} %constant.166) | copy-start | bytes 28
  24.9 39.7 %copy-start.13 = (s32[2]{0:T(128)S(1)}, s32[2]{0:T(128)}, u32[]{:S(2)}) copy-start(s32[2]{0:T(128)} %constant.163) | copy-start | bytes 28
  25.0 39.7 %copy-start.14 = (s32[2]{0:T(128)S(1)}, s32[2]{0:T(128)}, u32[]{:S(2)}) copy-start(s32[2]{0:T(128)} %constant.169) | copy-start | bytes 28
  25.0 69.8 %copy-start.1 = (f32[4,256,256]{2,1,0:T(8,128)S(1)}, f32[4,256,256]{2,1,0:T(8,128)}, u32[]{:S(2)}) copy-start(f32[4,256,256]{2,1,0:T(8,128)} %param.15) | copy-start | bytes 3145732
  86.0 8.4 %all-to-all-start.1 = ((s32[81,4,8]{0,2,1:T(8,128)}), s32[81,4,8]{0,2,1:T(8,128)S(1)}, u32[]{:S(2)}, u32[]{:S(2)}) async-start(s32[81,4,8]{0,2,1:T(8,128)} %copy.247), calls=%async_computation.1 | async-start | bytes 32768 | tf_op jit(solution)/shard_map/all_to_all | solution.py:20
  89.7 176.4 %all-gather.5.cloned.1.call-start = ((), (), s32[]{:S(2)}) async-start(), calls=%async_computation.10 | async-start | bytes 5242880 | tf_op jit(solution)/shard_map/all_gather | solution.py:62
  119.6 5.4 copy-start.5
  119.6 65.6 %all-to-all-start.2 = ((f32[8,81,4,1,256]{4,2,3,1,0:T(4,128)}), f32[8,81,4,1,256]{4,2,3,1,0:T(4,128)}, u32[]{:S(2)}, u32[]{:S(2)}) async-start(f32[8,81,4,1,256]{4,2,3,1,0:T(4,128)} %fusion.67), calls=%async_computation.2 | async-start | bytes 5308416 | tf_op jit(solution)/shard_map/all_to_all | solution.py:32
  124.2 163.7 %all-gather.7.cloned.1.call-start = ((), (), s32[]{:S(2)}) async-start(), calls=%async_computation.11 | async-start | bytes 5242880 | tf_op jit(solution)/shard_map/all_gather | solution.py:63
  189.0 37.2 %all-to-all-start.3 = ((f32[81,4,8,256]{3,2,0,1:T(8,128)}), f32[81,4,8,256]{3,2,0,1:T(8,128)}, u32[]{:S(2)}, u32[]{:S(2)}) async-start(f32[81,4,8,256]{3,2,0,1:T(8,128)} %copy.257), calls=%async_computation.3 | async-start | bytes 5308416 | tf_op jit(solution)/shard_map/all_to_all | solution.py:30
  193.7 6.5 %copy-start.11 = (s32[4,128]{1,0:T(4,128)S(1)}, s32[4,128]{1,0:T(4,128)}, u32[]{:S(2)}) copy-start(s32[4,128]{1,0:T(4,128)} %param.19) | copy-start | bytes 6148
  261.5 22.8 %all-to-all-start.4 = ((bf16[33,8,1024]{2,0,1:T(8,128)(2,1)}), bf16[33,8,1024]{2,0,1:T(8,128)(2,1)S(1)}, u32[]{:S(2)}, u32[]{:S(2)}) async-start(bf16[33,8,1024]{2,0,1:T(8,128)(2,1)} %copy.263), calls=%async_computation.4 | async-start | bytes 1310720 | tf_op jit(solution)/shard_map/all_to_all | solution.py:91
  287.9 3.9 copy-start.16
  292.9 21.6 %all-to-all-start.5 = ((bf16[33,8,1024]{2,0,1:T(8,128)(2,1)}), bf16[33,8,1024]{2,0,1:T(8,128)(2,1)S(1)}, u32[]{:S(2)}, u32[]{:S(2)}) async-start(bf16[33,8,1024]{2,0,1:T(8,128)(2,1)} %copy.265), calls=%async_computation.5 | async-start | bytes 1310720 | tf_op jit(solution)/shard_map/all_to_all | solution.py:98
  300.8 0.6 copy-start.6
  317.5 3.0 copy-start.4
  317.8 2.8 copy-start.3
  317.8 3.6 copy-start.12
  321.4 0.6 copy-start.9
  344.7 21.6 %all-to-all-start.6 = ((bf16[33,8,1024]{2,0,1:T(8,128)(2,1)}), bf16[33,8,1024]{2,0,1:T(8,128)(2,1)S(1)}, u32[]{:S(2)}, u32[]{:S(2)}) async-start(bf16[33,8,1024]{2,0,1:T(8,128)(2,1)} %copy.273), calls=%async_computation.6 | async-start | bytes 1310720 | tf_op jit(solution)/shard_map/all_to_all | solution.py:132
  373.9 21.6 %all-to-all-start.7 = ((bf16[33,8,1024]{2,0,1:T(8,128)(2,1)}), bf16[33,8,1024]{2,0,1:T(8,128)(2,1)S(1)}, u32[]{:S(2)}, u32[]{:S(2)}) async-start(bf16[33,8,1024]{2,0,1:T(8,128)(2,1)} %copy.275), calls=%async_computation.7 | async-start | bytes 1310720 | tf_op jit(solution)/shard_map/all_to_all | solution.py:143
  377.7 5.4 copy-start.7
  417.3 8.5 %copy-start.2 = (f32[2592,256]{1,0:T(8,128)S(1)}, f32[2592,256]{1,0:T(8,128)}, u32[]{:S(2)}) copy-start(f32[2592,256]{1,0:T(8,128)} %scatter_custom_fusion.6) | copy-start | bytes 7962628
  528.2 16.4 %copy-start.10 = (f32[4,256]{1,0:T(4,128)S(1)}, f32[4,256]{1,0:T(4,128)}, u32[]{:S(2)}) copy-start(f32[4,256]{1,0:T(4,128)} %param.16) | copy-start | bytes 12292
Sparse Core Ops, SparseCore 0:
  92.3 51.1 all-gather.4
  145.4 68.2 all-gather.6
